TPU v7x, 512 devices: a whole 4x4x16 slice. The times are simulated.
512 devices in a mesh: dp: 128 (over x_hi, y, z), fsdp: 4 (over x_lo, core).
Axes of the slice: x: 4 (x_hi: 2, x_lo: 2; x = x_hi * 2 + x_lo), y: 4, z: 16, core: 2. Of those that a mesh axis runs over, the one named last changes fastest.
Arguments:
- tokens: bfloat16 [65536, 1280], P(('dp', 'fsdp')), may hold values from -3 to 3
- qkv_weight: bfloat16 [3, 1280, 1280], P(None, 'dp', 'fsdp'), may hold values from -1 to 1
- out_weight: bfloat16 [1280, 1280], P('fsdp', 'dp'), may hold values from -0.15625 to 0.15625
- merge_weight: bfloat16 [5120, 1280], P(('dp', 'fsdp')), may hold values from -0.078125 to 0.078125
- ln_gains: float32 [2, 1280], replicated, may hold values from 0.25 to 1.75
- segments: int32 [128, 512], P('dp', 'fsdp'), may hold values from 0 to 2, never falling along the last dimension, each value on 1 to 256 neighbouring positions
- merge_rows: int32 [512, 128], P(('dp', 'fsdp')), may hold values from 0 to 127, each once within a row
- owners: int32 [16384, 1], P(('dp', 'fsdp')), may hold values from 0 to 127; in each aligned block of 32 rows (0 to 31, 32 to 63, ...) at most 2 rows name the same one
Outputs:
- owned: bfloat16 [131072, 1280], P(('dp', 'fsdp'))
Inputs may be any that keep to these rules, and one draw needn't show every extreme that they name: `segments`: within each row segment numbers never fall, every number appears, each request has 1 to 256 tokens and one has exactly 256. `merge_rows`: each row is a permutation of the device's local rows. `owners`: among the 32 merged tokens of one device no owner appears more than 2 times, and in some devices one appears exactly 2 times.
All inputs are finite; a program needn't handle non-finite values.
Results may differ from a plain program's by a relative error of at most 0.02.
Values may be sent and summed in bfloat16 or wider, within the bound.
A program may use at most 64 MiB of HBM per device.

v0:
```python
import math
import jax
import jax.numpy as jnp
from jax import lax
from jax.sharding import PartitionSpec as P

HD = 80
epsilon = 1e-06


def normalize(values_in, gain_row):
    widened = values_in.astype(jnp.float32)
    centered = widened - jnp.mean(widened, axis=1, keepdims=True)
    variance = jnp.mean(centered * centered, axis=1, keepdims=True)
    return (centered * lax.rsqrt(variance + epsilon) * gain_row).astype(jnp.bfloat16)


def attend(queries, keys_all, values_all, seg_rows, seg_cols):
    factor = 1.0 / math.sqrt(HD)
    allowed = seg_rows[:, None] == seg_cols[None, :]
    pieces = []
    for head_index in range(queries.shape[1] // HD):
        first_col = head_index * HD
        last_col = first_col + HD
        scores = (
            lax.dot_general(
                queries[:, first_col:last_col],
                keys_all[:, first_col:last_col],
                (((1,), (1,)), ((), ())),
                preferred_element_type=jnp.float32,
            )
            * factor
        )
        masked = jnp.where(allowed, scores, -jnp.inf)
        highest = jnp.max(masked, axis=1, keepdims=True)
        weights = jnp.exp(masked - highest)
        totals = jnp.sum(weights, axis=1, keepdims=True)
        head_out = jnp.dot(
            weights.astype(jnp.bfloat16),
            values_all[:, first_col:last_col],
            preferred_element_type=jnp.float32,
        )
        pieces.append(head_out / totals)
    return jnp.concatenate(pieces, axis=1).astype(jnp.bfloat16)


def per_device(
    tokens, qkv_weight, out_weight, merge_weight, ln_gains, segments, merge_rows, owners
):
    n_dp = lax.axis_size("dp")
    n_fsdp = lax.axis_size("fsdp")
    qkv_mine = lax.all_gather(qkv_weight, "dp", axis=1, tiled=True)
    out_mine = lax.all_gather(out_weight, "dp", axis=1, tiled=True)
    normed = normalize(tokens, ln_gains[0])
    group_normed, group_segs = (
        lax.all_gather(normed, "fsdp", axis=0, tiled=True),
        lax.all_gather(segments, "fsdp", axis=1, tiled=True),
    )
    queries = jnp.dot(group_normed, qkv_mine[0], preferred_element_type=jnp.float32).astype(
        jnp.bfloat16
    )
    keys_all = jnp.dot(group_normed, qkv_mine[1], preferred_element_type=jnp.float32).astype(
        jnp.bfloat16
    )
    values_all = jnp.dot(group_normed, qkv_mine[2], preferred_element_type=jnp.float32).astype(
        jnp.bfloat16
    )
    attended_mine = attend(queries, keys_all, values_all, group_segs[0], group_segs[0])
    attended_local = lax.all_to_all(attended_mine, "fsdp", split_axis=0, concat_axis=1, tiled=True)
    out_full = lax.all_gather(out_mine, "fsdp", axis=0, tiled=True)
    update = jnp.dot(attended_local, out_full, preferred_element_type=jnp.float32)
    layer_out = (tokens.astype(jnp.float32) + update).astype(jnp.bfloat16)
    merge_in = normalize(layer_out, ln_gains[1])
    merge_count = tokens.shape[0] // 4
    stacked = jnp.take(merge_in, merge_rows[0], axis=0).reshape(merge_count, 4 * merge_in.shape[1])
    slice_rows = merge_weight.shape[0]
    part_rows = lax.all_gather(merge_weight, "dp", axis=0, tiled=True)
    blocks = stacked.reshape(merge_count, n_dp, n_fsdp * slice_rows)
    received = lax.all_to_all(blocks, "fsdp", split_axis=2, concat_axis=0, tiled=True)
    gathered_inputs = received.reshape(n_fsdp * merge_count, n_dp * slice_rows)
    merged = lax.psum_scatter(
        jnp.dot(gathered_inputs, part_rows, preferred_element_type=jnp.float32).astype(
            jnp.bfloat16
        ),
        "fsdp",
        scatter_dimension=0,
        tiled=True,
    )
    capacity = max(2, (2 * merge_count + n_dp - 1) // n_dp)
    targets = owners[:, 0]
    onehot = (targets[:, None] == jnp.arange(n_dp, dtype=jnp.int32)[None, :]).astype(jnp.int32)
    earlier = jnp.cumsum(onehot, axis=0) - onehot
    position = jnp.sum(earlier * onehot, axis=1)
    slot_index = targets * capacity + position
    placing = (jnp.arange(n_dp * capacity, dtype=jnp.int32)[:, None] == slot_index[None, :]).astype(
        jnp.bfloat16
    )
    packed = jnp.dot(placing, merged, preferred_element_type=jnp.float32).astype(jnp.bfloat16)
    packed = packed.reshape(n_dp, capacity, merged.shape[1])
    arrived = lax.all_to_all(packed, "dp", split_axis=0, concat_axis=0, tiled=True)
    return arrived.reshape(n_dp * capacity, merged.shape[1])


def solution(mesh):
    return jax.shard_map(
        per_device,
        mesh=mesh,
        in_specs=(
            P(("dp", "fsdp"), None),
            P(None, "dp", "fsdp"),
            P("fsdp", "dp"),
            P(("dp", "fsdp"), None),
            P(),
            P("dp", "fsdp"),
            P(("dp", "fsdp"), None),
            P(("dp", "fsdp"), None),
        ),
        out_specs=P(("dp", "fsdp"), None),
        check_vma=False,
    )
```

profile of v0, /device:TPU:32, one launch (start us, length us, event | category | flops | bytes accessed | tf_op | source)
XLA Modules:
  0.0 750.7 jit_solution(5897725297791308447)
XLA Ops:
  6.5 0.7 all-gather.9.cloned.1.call-update
  7.3 0.8 slice_reduce_fusion
  8.1 1.1 convert_reduce_fusion
  9.2 1.2 fusion.23
  10.4 1.9 fusion.25
  12.4 364.9 %all-gather = bf16[128,10,320]{2,1,0:T(8,128)(2,1)S(1)} all-gather(bf16[1,10,320]{2,1,0:T(8,128)(2,1)} %bitcast.57), channel_id=1, replica_groups=mesh['dp'=128,'fsdp'=4] {'dp'}, dimensions={0}, use_global_device_ids=true | all-gather | bytes 825600 | tf_op jit(solution)/shard_map/all_gather | solution.py:53
  377.3 0.6 reshape.112
  378.0 1.3 copy.23
  379.4 0.5 all-gather.13.cloned.1.call-update
  379.9 5.0 all_gather.18
  384.9 0.5 broadcast.113
  385.5 0.6 reduce.7
  386.5 10.5 %fusion.49 = (bf16[1,1280,320]{2,0,1:T(2,128)(2,1)S(1)}, bf16[1,1280,320]{2,0,1:T(2,128)(2,1)}, bf16[1,1280,320]{2,0,1:T(2,128)(2,1)}) fusion(bf16[3,1280,320]{2,0,1:T(4,128)(2,1)} %all-gather.9.cloned.1.call-done), kind=kLoop, calls=%fused_computation.92 | loop fusion | bytes 4915200 | tf_op jit(solution)/shard_map/slice | solution.py:65
  396.9 4.9 copy.28
  401.8 4.9 copy.27
  406.7 2.8 copy.26
  409.5 2.3 convolution_convert_fusion.3
  411.9 0.6 convolution_convert_fusion.4
  412.5 0.4 fusion.53
  413.1 0.4 fusion.52
  413.6 0.4 fusion.51
  414.2 0.4 fusion.50
  414.8 0.6 convolution_convert_fusion.2
  415.4 0.3 fusion.9
  415.7 0.3 fusion.8
  416.0 0.3 fusion.7
  416.3 0.3 fusion.6
  416.7 0.7 pad_maximum_fusion
  417.5 3.5 all-to-all-start
  420.9 0.2 reduce-scatter.2.cloned.1.call-start
  421.2 6.4 all-to-all-done
  427.6 2.6 fusion.54
  430.3 0.2 multiply_reduce_fusion
  430.7 0.9 gather_fusion
  431.6 1.9 gather.7
  433.5 0.7 broadcast_select_fusion
  434.2 0.6 copy.24
  434.8 9.1 %all_to_all.36 = bf16[32,128,40]{1,0,2:T(8,128)(2,1)S(1)} all-to-all(bf16[32,128,40]{1,0,2:T(8,128)(2,1)S(1)} %copy.24), channel_id=1, replica_groups=mesh['dp'=128,'fsdp'=4] {'fsdp'}, dimensions={2} | all-to-all | bytes 655360 | tf_op jit(solution)/shard_map/all_to_all | solution.py:79
  443.9 0.8 copy.25
  444.7 1.4 reshape.100
  446.1 210.0 %all-gather.13.cloned.1.call-done = bf16[128,10,1280]{2,1,0:T(8,128)(2,1)} async-done(((bf16[1,10,1280]{2,1,0:T(8,128)(2,1)}), bf16[128,10,1280]{2,1,0:T(8,128)(2,1)}) %all-gather.13.cloned.1.call-update) | async-done | bytes 3276816 | tf_op jit(solution)/shard_map/all_gather | solution.py:77
  656.1 5.3 reshape.114
  661.4 2.3 convolution_convert_fusion.1
  664.1 19.2 %reduce-scatter.2.cloned.1.call-done = bf16[32,1280]{1,0:T(8,128)(2,1)} async-done(((bf16[128,1280]{1,0:T(8,128)(2,1)}), bf16[32,1280]{1,0:T(8,128)(2,1)}) %reduce-scatter.2.cloned.1.call-update) | async-done | bytes 81936 | tf_op jit(solution)/shard_map/reduce_scatter | solution.py:81
  683.3 1.2 convolution_convert_fusion
  684.5 0.2 reshape.101
  684.7 58.4 %all_to_all.37 = bf16[128,2,1280]{2,1,0:T(2,128)(2,1)S(1)} all-to-all(bf16[128,2,1280]{2,1,0:T(2,128)(2,1)S(1)} %reshape.101), channel_id=1, replica_groups=mesh['dp'=128,'fsdp'=4] {'dp'}, dimensions={0} | all-to-all | bytes 1310720 | tf_op jit(solution)/shard_map/all_to_all | solution.py:100
  743.1 1.1 reshape.102
  (43 shorter events, 1.9 us)
Async XLA Ops:
  6.5 379.9 %all-gather.9.cloned.1.call-start = ((), (), s32[]{:S(2)}) async-start(), calls=%async_computation.5 | async-start | bytes 3962880 | tf_op jit(solution)/shard_map/all_gather | solution.py:52
  7.3 402.2 %all-gather.7.cloned.1.call-start = ((), (), s32[]{:S(2)}) async-start(), calls=%async_computation.4 | async-start | bytes 1638400 | tf_op jit(solution)/shard_map/all_gather | solution.py:56
  12.4 408.8 %all-gather.11.cloned.1.call-start = ((), (), s32[]{:S(2)}) async-start(), calls=%async_computation.6 | async-start | bytes 4096000 | tf_op jit(solution)/shard_map/all_gather | solution.py:70
  378.0 1.9 copy-start.3
  378.0 7.5 copy-start.5
  379.3 276.8 %all-gather.13.cloned.1.call-start = ((), (), s32[]{:S(2)}) async-start(), calls=%async_computation.8 | async-start | bytes 5283840 | tf_op jit(solution)/shard_map/all_gather | solution.py:77
  409.4 2.4 copy-start.1
  409.5 2.4 copy-start.4
  416.0 11.6 %copy-start = (bf16[128,1280]{1,0:T(8,128)(2,1)S(1)}, bf16[128,1280]{1,0:T(8,128)(2,1)}, u32[]{:S(2)}) copy-start(bf16[128,1280]{1,0:T(8,128)(2,1)} %param.8) | copy-start | bytes 983044
  417.5 10.2 %all-to-all-start = ((bf16[4,128,320]{1,2,0:T(8,128)(2,1)}), bf16[4,128,320]{1,2,0:T(8,128)(2,1)S(1)}, u32[]{:S(2)}, u32[]{:S(2)}) async-start(bf16[4,128,320]{1,2,0:T(8,128)(2,1)} %pad_maximum_fusion), calls=%async_computation | async-start | bytes 655360 | tf_op jit(solution)/shard_map/all_to_all | solution.py:69
  420.9 262.3 %reduce-scatter.2.cloned.1.call-start = ((), (), s32[]{:S(2)}) async-start(), calls=%async_computation.7 | async-start | bytes 409600 | tf_op jit(solution)/shard_map/reduce_scatter | solution.py:81
  661.4 2.4 copy-start.2
Sparse Core Ops, SparseCore 0:
  11.8 226.8 all-gather.8
  240.8 25.3 all-gather.6
  379.4 39.2 all-gather.10
  422.9 233.0 all-gather.12
  663.8 19.3 reduce-scatter.1
where the time goes:
time: 752 us; the launch traced here: 751 us
  blocking collectives  437 us (58%)
  waiting for transfers between devices  237 us (32%)
  local copies, waits for them, and re-layouts  38.7 us (5%)
  between operations  13.5 us (2%)
  matrix products  12.4 us (2%)
  other arithmetic  7.87 us (1%)
    all_gather x1, blocking collectives, per_device(): out_mine = lax.all_gather(out_weight, 'dp', axis=1, tiled=True)  365 us
    all_gather x1, waiting for transfers between devices, per_device(): part_rows = lax.all_gather(merge_weight, 'dp', axis=0, tiled=True)  210 us
    all_to_all x1, blocking collectives, per_device(): lax.all_to_all(packed, 'dp', split_axis=0, concat_axis=0, tiled=True)  58.4 us
    unnamed x19, local copies, waits for them, and re-layouts  20.2 us
    reduce_scatter x1, waiting for transfers between devices, per_device(): lax.psum_scatter(jnp.dot(gathered_inputs, part_rows, preferred_element_ty...  19.2 us
  transfers between devices with their start and end apart: 6, of which 3 were waited for; matrix products, arithmetic and copies ran while one was open for 7% of the time, Pallas kernels for 0%

commit v1 on v0

--- a/solution.py
+++ b/solution.py
@@ -50,7 +50,10 @@
     n_dp = lax.axis_size("dp")
     n_fsdp = lax.axis_size("fsdp")
     qkv_mine = lax.all_gather(qkv_weight, "dp", axis=1, tiled=True)
-    out_mine = lax.all_gather(out_weight, "dp", axis=1, tiled=True)
+    count = lax.axis_size("dp")
+    parts = jnp.stack([out_weight for _ in range(count)])
+    parts = lax.all_to_all(parts, "dp", split_axis=0, concat_axis=0)
+    out_mine = jnp.concatenate(parts, axis=1)
     normed = normalize(tokens, ln_gains[0])
     group_normed, group_segs = (
         lax.all_gather(normed, "fsdp", axis=0, tiled=True),

time: 752 us -> 659 us (0.88)
  blocking collectives: 437 us -> 63.4 us
  waiting for transfers between devices: 237 us -> 491 us
  starting transfers between devices: 3.8 us -> 29.7 us
    all_gather x1 -> x0, blocking collectives: 365 us -> none  [per_device(): out_mine = lax.all_gather(out_weight, 'dp', axis=1, tiled=True)]
    all_gather x1, waiting for transfers between devices: 0.02 us -> 130 us  [per_device(): qkv_mine = lax.all_gather(qkv_weight, 'dp', axis=1, tiled=True)]
    all_to_all x0 -> x2, waiting for transfers between devices: none -> 76.4 us  [the longest x1 76.4 us: per_device(): parts = lax.all_to_all(parts, 'dp', split_axis=0, concat_axis=0)]
    all_gather x1, waiting for transfers between devices: 0.02 us -> 31.4 us  [per_device(): out_full = lax.all_gather(out_mine, 'fsdp', axis=0, tiled=True)]
    all_to_all x0 -> x2, starting transfers between devices: none -> 25.9 us  [the longest x1 21.8 us: per_device(): parts = lax.all_to_all(parts, 'dp', split_axis=0, concat_axis=0)]
    all_gather x1, waiting for transfers between devices: 210 us -> 222 us  [per_device(): part_rows = lax.all_gather(merge_weight, 'dp', axis=0, tiled=True)]
    all_to_all x1 -> x0, blocking collectives: 9.11 us -> none  [per_device(): lax.all_to_all(blocks, 'fsdp', split_axis=2, concat_axis=0, tiled=True)]
  transfers between devices with their start and end apart: 6 -> 8, of which waited for: 3 -> 7; matrix products, arithmetic and copies ran while one was open for 7% -> 8% of each run, Pallas kernels for 0% -> 0%
where the time goes in v1:
time: 659 us; the launch traced here: 658 us
  waiting for transfers between devices  491 us (75%)
  blocking collectives  63.4 us (10%)
  local copies, waits for them, and re-layouts  43.7 us (7%)
  starting transfers between devices  29.7 us (5%)
  between operations  13.5 us (2%)
  matrix products  12.3 us (2%)
    all_gather x1, waiting for transfers between devices, per_device(): part_rows = lax.all_gather(merge_weight, 'dp', axis=0, tiled=True)  222 us
    all_gather x1, waiting for transfers between devices, per_device(): qkv_mine = lax.all_gather(qkv_weight, 'dp', axis=1, tiled=True)  130 us
    all_to_all x1, waiting for transfers between devices, per_device(): parts = lax.all_to_all(parts, 'dp', split_axis=0, concat_axis=0)  76.4 us
    all_to_all x1, blocking collectives, per_device(): lax.all_to_all(packed, 'dp', split_axis=0, concat_axis=0, tiled=True)  58.4 us
    all_gather x1, waiting for transfers between devices, per_device(): out_full = lax.all_gather(out_mine, 'fsdp', axis=0, tiled=True)  31.4 us
    all_to_all x1, starting transfers between devices, per_device(): parts = lax.all_to_all(parts, 'dp', split_axis=0, concat_axis=0)  21.8 us
    reduce_scatter x1, waiting for transfers between devices, per_device(): lax.psum_scatter(jnp.dot(gathered_inputs, part_rows, preferred_element_ty...  19.2 us
    unnamed x19, local copies, waits for them, and re-layouts  18.4 us
  transfers between devices with their start and end apart: 8, of which 7 were waited for; matrix products, arithmetic and copies ran while one was open for 8% of the time, Pallas kernels for 0%

profile of v1, /device:TPU:32, one launch (start us, length us, event | category | flops | bytes accessed | tf_op | source)
XLA Modules:
  0.0 658.4 jit_solution(1961856393388038050)
XLA Ops:
  6.5 0.7 all-gather.8.cloned.1.call-update
  7.3 2.0 stack.2
  9.3 21.8 %all-to-all-start.1 = ((bf16[128,320,10]{1,2,0:T(8,128)(2,1)}), bf16[128,320,10]{1,2,0:T(8,128)(2,1)S(1)}, u32[]{:S(2)}, u32[]{:S(2)}) async-start(bf16[128,320,10]{1,2,0:T(8,128)(2,1)} %stack.2), calls=%async_computation.1 | async-start | bytes 3145728 | tf_op jit(solution)/shard_map/all_to_all | solution.py:55
  31.5 1.0 fusion.25
  32.6 76.4 %all-to-all-done.1 = bf16[128,320,10]{1,2,0:T(8,128)(2,1)S(1)} async-done(((bf16[128,320,10]{1,2,0:T(8,128)(2,1)}), bf16[128,320,10]{1,2,0:T(8,128)(2,1)S(1)}, u32[]{:S(2)}, u32[]{:S(2)}) %all-to-all-start.1) | async-done | bytes 819232 | tf_op jit(solution)/shard_map/all_to_all | solution.py:55
  108.9 0.6 reshape.109
  109.6 1.3 copy.24
  110.9 0.5 all-gather.12.cloned.1.call-update
  111.5 5.0 all_gather.15
  116.5 0.5 broadcast.115
  117.0 0.6 reduce.7
  118.0 130.0 %all-gather.8.cloned.1.call-done = bf16[3,1280,320]{2,0,1:T(4,128)(2,1)} async-done(((bf16[3,10,320]{2,0,1:T(4,128)(2,1)}), bf16[3,1280,320]{2,0,1:T(4,128)(2,1)}) %all-gather.8.cloned.1.call-update) | async-done | bytes 2457616 | tf_op jit(solution)/shard_map/all_gather | solution.py:52
  248.0 10.5 %fusion.49 = (bf16[1,1280,320]{2,0,1:T(2,128)(2,1)S(1)}, bf16[1,1280,320]{2,0,1:T(2,128)(2,1)}, bf16[1,1280,320]{2,0,1:T(2,128)(2,1)}) fusion(bf16[3,1280,320]{2,0,1:T(4,128)(2,1)} %all-gather.8.cloned.1.call-done), kind=kLoop, calls=%fused_computation.92 | loop fusion | bytes 4915200 | tf_op jit(solution)/shard_map/slice | solution.py:68
  258.5 4.9 copy.29
  263.4 4.9 copy.28
  268.3 2.8 copy.27
  271.0 4.0 all-gather.6.cloned.1.call-done
  275.0 2.3 convolution_convert_fusion.3
  277.3 0.6 convolution_convert_fusion.4
  277.9 0.4 fusion.53
  278.5 0.4 fusion.52
  279.1 0.4 fusion.51
  279.7 0.4 fusion.50
  280.2 0.6 convolution_convert_fusion.2
  280.8 0.3 fusion.9
  281.1 0.3 fusion.8
  281.5 0.3 fusion.7
  281.8 0.3 fusion.6
  282.1 0.7 pad_maximum_fusion
  282.9 3.6 all-to-all-start
  286.6 6.5 all-to-all-done
  293.1 31.4 %all-gather.10.cloned.1.call-done = bf16[1280,1280]{1,0:T(8,128)(2,1)} async-done(((bf16[320,1280]{1,0:T(8,128)(2,1)}), bf16[1280,1280]{1,0:T(8,128)(2,1)}) %all-gather.10.cloned.1.call-update) | async-done | bytes 3276816 | tf_op jit(solution)/shard_map/all_gather | solution.py:73
  324.4 2.6 fusion.54
  327.5 0.9 gather_fusion
  328.4 1.9 gather.7
  330.3 0.7 broadcast_select_fusion
  331.0 1.3 copy.25
  332.3 4.1 all-to-all-start.2
  336.5 222.1 %all-gather.12.cloned.1.call-done = bf16[128,10,1280]{2,1,0:T(8,128)(2,1)} async-done(((bf16[1,10,1280]{2,1,0:T(8,128)(2,1)}), bf16[128,10,1280]{2,1,0:T(8,128)(2,1)}) %all-gather.12.cloned.1.call-update) | async-done | bytes 3276816 | tf_op jit(solution)/shard_map/all_gather | solution.py:80
  558.6 5.3 reshape.122
  563.9 2.4 copy.26
  566.3 2.7 reshape.110
  569.1 2.3 convolution_convert_fusion.1
  571.8 19.2 %reduce-scatter.2.cloned.1.call-done = bf16[32,1280]{1,0:T(8,128)(2,1)} async-done(((bf16[128,1280]{1,0:T(8,128)(2,1)}), bf16[32,1280]{1,0:T(8,128)(2,1)}) %reduce-scatter.2.cloned.1.call-update) | async-done | bytes 81936 | tf_op jit(solution)/shard_map/reduce_scatter | solution.py:84
  591.0 1.2 convolution_convert_fusion
  592.2 0.2 reshape.111
  592.4 58.4 %all_to_all.41 = bf16[128,2,1280]{2,1,0:T(2,128)(2,1)S(1)} all-to-all(bf16[128,2,1280]{2,1,0:T(2,128)(2,1)S(1)} %reshape.111), channel_id=1, replica_groups=mesh['dp'=128,'fsdp'=4] {'dp'}, dimensions={0} | all-to-all | bytes 1310720 | tf_op jit(solution)/shard_map/all_to_all | solution.py:103
  650.8 1.1 reshape.112
  (48 shorter events, 2.5 us)
Async XLA Ops:
  6.5 241.5 %all-gather.8.cloned.1.call-start = ((), (), s32[]{:S(2)}) async-start(), calls=%async_computation.6 | async-start | bytes 3962880 | tf_op jit(solution)/shard_map/all_gather | solution.py:52
  9.3 21.8 %copy-start.2 = (f32[2,1280]{1,0:T(2,128)S(1)}, f32[2,1280]{1,0:T(2,128)}, u32[]{:S(2)}) copy-start(f32[2,1280]{1,0:T(2,128)} %param.12) | copy-start | bytes 30724
  9.3 21.9 %copy-start = (bf16[128,1280]{1,0:T(8,128)(2,1)S(1)}, bf16[128,1280]{1,0:T(8,128)(2,1)}, u32[]{:S(2)}) copy-start(bf16[128,1280]{1,0:T(8,128)(2,1)} %param.8) | copy-start | bytes 983044
  9.3 99.7 %all-to-all-start.1 = ((bf16[128,320,10]{1,2,0:T(8,128)(2,1)}), bf16[128,320,10]{1,2,0:T(8,128)(2,1)S(1)}, u32[]{:S(2)}, u32[]{:S(2)}) async-start(bf16[128,320,10]{1,2,0:T(8,128)(2,1)} %stack.2), calls=%async_computation.1 | async-start | bytes 3145728 | tf_op jit(solution)/shard_map/all_to_all | solution.py:55
  31.0 244.0 %all-gather.6.cloned.1.call-start = ((), (), s32[]{:S(2)}) async-start(), calls=%async_computation.5 | async-start | bytes 1638400 | tf_op jit(solution)/shard_map/all_gather | solution.py:59
  32.5 291.9 %all-gather.10.cloned.1.call-start = ((), (), s32[]{:S(2)}) async-start(), calls=%async_computation.7 | async-start | bytes 4096000 | tf_op jit(solution)/shard_map/all_gather | solution.py:73
  109.6 1.9 copy-start.4
  109.6 7.5 %copy-start.6 = (s32[1,128]{1,0:T(1,128)S(1)}, s32[1,128]{1,0:T(1,128)}, u32[]{:S(2)}) copy-start(s32[1,128]{1,0:T(1,128)} %param.14) | copy-start | bytes 1540
  110.9 447.7 %all-gather.12.cloned.1.call-start = ((), (), s32[]{:S(2)}) async-start(), calls=%async_computation.9 | async-start | bytes 5283840 | tf_op jit(solution)/shard_map/all_gather | solution.py:80
  271.0 6.3 copy-start.1
  275.0 2.3 copy-start.5
  282.9 10.2 %all-to-all-start = ((bf16[4,128,320]{1,2,0:T(8,128)(2,1)}), bf16[4,128,320]{1,2,0:T(8,128)(2,1)S(1)}, u32[]{:S(2)}, u32[]{:S(2)}) async-start(bf16[4,128,320]{1,2,0:T(8,128)(2,1)} %pad_maximum_fusion), calls=%async_computation | async-start | bytes 655360 | tf_op jit(solution)/shard_map/all_to_all | solution.py:72
  332.3 231.6 %all-to-all-start.2 = ((bf16[32,128,40]{1,0,2:T(8,128)(2,1)}), bf16[32,128,40]{1,0,2:T(8,128)(2,1)}, u32[]{:S(2)}, u32[]{:S(2)}) async-start(bf16[32,128,40]{1,0,2:T(8,128)(2,1)} %copy.25), calls=%async_computation.2 | async-start | bytes 655360 | tf_op jit(solution)/shard_map/all_to_all | solution.py:82
  336.4 254.5 %reduce-scatter.2.cloned.1.call-start = ((), (), s32[]{:S(2)}) async-start(), calls=%async_computation.8 | async-start | bytes 409600 | tf_op jit(solution)/shard_map/reduce_scatter | solution.py:84
  569.1 2.4 copy-start.3
Sparse Core Ops, SparseCore 0:
  11.8 236.1 all-gather.7
  250.1 24.8 all-gather.5
  277.1 47.2 all-gather.9
  328.7 229.8 all-gather.11
  571.5 19.3 reduce-scatter.1
